TPU v7x, 32 devices: a whole 2x2x4 slice. The times are simulated.
32 devices in a mesh: scen: 8 (over z, core), dec: 4 (over y, x).
Axes of the slice: x: 2, y: 2, z: 4, core: 2. Of those that a mesh axis runs over, the one named last changes fastest.
Arguments:
- order_qty: bfloat16 [8192, 4096], P('dec', 'scen'), may hold values from 0 to 2
- multiplier: float32 [8192, 4096], P('dec', 'scen'), may hold values from -6 to 6
- unit_cost: bfloat16 [8192, 4096], P('dec', 'scen'), may hold values from -6 to 6
- demand: bfloat16 [2048, 4096], P('dec', 'scen'), may hold values from -6 to 6
- technology: bfloat16 [8192, 2048], P('dec'), may hold values from -0.0625 to 0.0625
- kkt_inverse: bfloat16 [2048, 2048], P('dec'), may hold values from -1 to 3
- probability: float32 [4096], P('scen'), may hold values from 0.1 to 1
- scenario_node: int32 [4096, 1], P('scen'), may hold values from 0 to 511
Outputs:
- planned: bfloat16 [8192, 4096], P('dec', 'scen')
- recourse: bfloat16 [2048, 4096], P('dec', 'scen')
- consensus: float32 [8192, 512], P('dec')
- multiplier_next: float32 [8192, 4096], P('dec', 'scen')
Inputs may be any that keep to these rules, and one draw needn't show every extreme that they name: `scenario_node`: every one of the 512 nodes is the node of some scenario.
All inputs are finite; a program needn't handle non-finite values.
Results may differ from a plain program's by a relative error of at most 0.023.
Values may be sent and summed in bfloat16 or wider, within the bound.
No kernel may reach another device: no remote copies, remote signals or barrier semaphores. Data moves between devices by JAX's collectives and lax.ppermute only.
A program may use at most 128 MiB of HBM per device.

v0:
```python
import jax
import jax.numpy as jnp
from jax import lax
from jax.sharding import PartitionSpec as P

G = 512
step_size = 0.5
penalty = 2.0


def on_device(
    order_qty, multiplier, unit_cost, demand, technology, kkt_inverse, probability, scenario_node
):
    contract_first = (((0,), (0,)), ((), ()))
    columns = technology
    supply = lax.psum_scatter(
        lax.dot_general(columns, order_qty, contract_first, preferred_element_type=jnp.float32),
        "dec",
        scatter_dimension=0,
        tiled=True,
    )
    right_side = (demand.astype(jnp.float32) - supply).astype(jnp.bfloat16)
    columns = kkt_inverse
    solved = jnp.dot(
        columns,
        lax.all_gather(right_side, "dec", axis=0, tiled=True),
        preferred_element_type=jnp.float32,
    )
    recourse = solved.astype(jnp.bfloat16)
    columns = technology
    linked = jnp.dot(
        columns,
        lax.all_gather(recourse, "dec", axis=0, tiled=True),
        preferred_element_type=jnp.float32,
    )
    gradient = unit_cost.astype(jnp.float32) + multiplier + linked
    planned = jnp.maximum(order_qty.astype(jnp.float32) - step_size * gradient, 0.0).astype(
        jnp.bfloat16
    )
    node_list = scenario_node[:, 0]
    node_ids = jnp.arange(G, dtype=jnp.int32)
    member = (node_list[:, None] == node_ids[None, :]).astype(jnp.float32)
    weight_table = member * probability[:, None]
    weight_high = weight_table.astype(jnp.bfloat16)
    weight_low = (weight_table - weight_high.astype(jnp.float32)).astype(jnp.bfloat16)
    totals = jnp.dot(planned, weight_high, preferred_element_type=jnp.float32)
    totals = totals + jnp.dot(planned, weight_low, preferred_element_type=jnp.float32)
    masses = jnp.dot(probability, member, precision=lax.Precision.HIGHEST)
    totals, masses = (
        lax.psum(totals.astype(jnp.bfloat16), "scen").astype(jnp.float32),
        lax.psum(masses.astype(jnp.bfloat16), "scen").astype(jnp.float32),
    )
    consensus = totals / masses[None, :]
    spread_back = jnp.take(consensus, node_list, axis=1)
    multiplier_next = multiplier + penalty * (planned.astype(jnp.float32) - spread_back)
    return (planned, recourse, consensus, multiplier_next)


def solution(mesh):
    placed = (
        P("dec", "scen"),
        P("dec", "scen"),
        P("dec", "scen"),
        P("dec", "scen"),
        P("dec", None),
        P("dec", None),
        P("scen"),
        P("scen", None),
    )
    return jax.shard_map(
        on_device,
        mesh=mesh,
        in_specs=placed,
        out_specs=(P("dec", "scen"), P("dec", "scen"), P("dec", None), P("dec", "scen")),
        check_vma=False,
    )
```

profile of v0, /device:TPU:0, one launch (start us, length us, event | category | flops | bytes accessed | tf_op | source)
XLA Modules:
  0.0 267.7 jit_solution(8834524278029128329)
XLA Ops:
  7.2 0.0 copy-start
  7.2 0.0 reduce-scatter.2.cloned.1.call-start
  7.2 10.7 %fusion.20 = f32[2048,512]{1,0:T(8,128)} fusion(bf16[2048,2048]{1,0:T(8,128)(2,1)} %param.12, bf16[2048,512]{1,0:T(8,128)(2,1)} %param.8), kind=kOutput, calls=%fused_computation.32 | convolution fusion | flops 4294967296 | bytes 14680064 | tf_op jit(solution)/shard_map/dot_general | solution.py:17
  17.9 0.0 copy-start.5
  17.9 0.0 reduce-scatter.2.cloned.1.call-update
  17.9 0.0 all-gather.3.cloned.1.call-start
  18.0 55.5 %reduce-scatter.2.cloned.1.call-done = f32[512,512]{1,0:T(8,128)} async-done(((f32[2048,512]{1,0:T(8,128)}), f32[512,512]{1,0:T(8,128)}) %reduce-scatter.2.cloned.1.call-update) | async-done | bytes 1048592 | tf_op jit(solution)/shard_map/reduce_scatter | solution.py:16
  73.4 0.0 copy-done.5
  73.4 2.2 subtract_convert_fusion
  75.6 0.0 all-gather.3.cloned.1.call-update
  75.7 0.0 all-gather.5.cloned.1.call-start
  75.7 35.4 %all-gather.3.cloned.1.call-done = bf16[2048,512]{1,0:T(8,128)(2,1)} async-done(((bf16[512,512]{1,0:T(8,128)(2,1)}), bf16[2048,512]{1,0:T(8,128)(2,1)}) %all-gather.3.cloned.1.call-update) | async-done | bytes 2097168 | tf_op jit(solution)/shard_map/all_gather | solution.py:26
  111.1 0.0 copy-done
  111.1 3.7 %fusion.6 = bf16[512,512]{0,1:T(8,128)(2,1)} fusion(bf16[2048,512]{1,0:T(8,128)(2,1)} %all-gather.3.cloned.1.call-done, bf16[512,2048]{1,0:T(8,128)(2,1)S(1)} %copy-done), kind=kOutput, calls=%fused_computation.14 | convolution fusion | flops 1074003968 | bytes 4718592 | tf_op jit(solution)/shard_map/dot_general | solution.py:24
  114.7 0.0 all-gather.5.cloned.1.call-update
  114.8 0.2 all-reduce.2.cloned.1.call-start
  115.0 3.9 %copy.12 = bf16[2048,512]{0,1:T(8,128)(2,1)} copy(bf16[2048,512]{1,0:T(8,128)(2,1)} %param.8) | data formatting | bytes 4194304 | tf_op args[0]
  118.9 0.0 copy-start.3
  118.9 5.6 %copy.14 = f32[2048,512]{0,1:T(8,128)} copy(f32[2048,512]{1,0:T(8,128)} %param.9) | data formatting | bytes 8388608 | tf_op args[1]
  124.5 0.0 copy-done.3
  124.5 2.4 copy.13
  126.8 0.0 copy-start.6
  126.8 0.0 copy-start.7
  126.9 23.1 %all-gather.5.cloned.1.call-done = bf16[2048,512]{0,1:T(8,128)(2,1)} async-done(((bf16[512,512]{0,1:T(8,128)(2,1)}), bf16[2048,512]{0,1:T(8,128)(2,1)}) %all-gather.5.cloned.1.call-update) | async-done | bytes 2097168 | tf_op jit(solution)/shard_map/all_gather | solution.py:33
  150.0 11.3 %fusion.5 = bf16[2048,512]{0,1:T(8,128)(2,1)S(1)} fusion(f32[2048,512]{0,1:T(8,128)} %copy.14, bf16[2048,512]{0,1:T(8,128)(2,1)} %copy.13, bf16[2048,512]{0,1:T(8,128)(2,1)} %copy.12, bf16[2048,512]{0,1:T(8,128)(2,1)} %all-gather.5.cloned.1.call-done, bf16[2048,2048]{1,0:T(8,128)(2,1)} %param.12), kind=kOutput, calls=%fused_computation.8 | convolution fusion | flops 4303355904 | bytes 20971520 | tf_op jit(solution)/shard_map/dot_general | solution.py:31
  161.3 0.0 copy-start.2
  161.3 0.0 copy-done.6
  161.3 0.0 copy-done.7
  161.3 1.4 fusion.9
  162.7 0.0 copy-start.4
  162.7 2.8 %add_convert_fusion = bf16[2048,512]{1,0:T(8,128)(2,1)} fusion(f32[2048,512]{1,0:T(8,128)S(1)} %fusion.9, bf16[2048,512]{0,1:T(8,128)(2,1)S(1)} %fusion.5, f32[512]{0:T(512)S(1)} %copy-done.7, s32[512]{0:T(512)S(1)} %bitcast.33), kind=kOutput, calls=%fused_computation.10 | convolution fusion | flops 1077411840 | bytes 8392704 | tf_op jit(solution)/shard_map/dot_general | solution.py:47
  165.5 0.0 all-reduce.2.cloned.1.call-update
  165.6 0.5 fusion.8
  166.1 16.8 %psum.15 = bf16[512]{0:T(512)(128)(2,1)S(1)} all-reduce(bf16[512]{0:T(512)(128)(2,1)S(1)} %convert_element_type.58), channel_id=1, replica_groups=mesh['scen'=8,'dec'=4] {'scen'}, use_global_device_ids=true, to_apply=%region_2.0 | all-reduce | flops 512 | bytes 2048 | tf_op jit(solution)/shard_map/psum | solution.py:51
  182.9 0.0 copy-done.4
  182.9 1.0 copy.18
  184.0 0.0 copy-done.2
  184.0 2.5 copy.17
  186.4 44.3 %all-reduce.2.cloned.1.call-done = bf16[2048,512]{1,0:T(8,128)(2,1)} async-done(((bf16[2048,512]{1,0:T(8,128)(2,1)}), bf16[2048,512]{1,0:T(8,128)(2,1)}) %all-reduce.2.cloned.1.call-update) | async-done | bytes 2097168 | tf_op jit(solution)/shard_map/psum | solution.py:50
  230.8 4.2 %convert_divide_fusion = f32[2048,512]{1,0:T(8,128)} fusion(bf16[2048,512]{1,0:T(8,128)(2,1)} %all-reduce.2.cloned.1.call-done, f32[512]{0:T(512)S(1)} %convert_element_type.59), kind=kLoop, calls=%fused_computation.9 | loop fusion | flops 2097152 | bytes 6293504 | tf_op jit(solution)/shard_map/div | solution.py:53
  235.0 5.5 %copy.15 = f32[2048,512]{0,1:T(8,128)} copy(f32[2048,512]{1,0:T(8,128)} %convert_divide_fusion) | data formatting | bytes 8388608 | tf_op jit(solution)/shard_map/div | solution.py:53
  240.5 7.6 %gather_fusion = f32[512,2048]{1,0:T(8,128)} fusion(f32[2048,512]{0,1:T(8,128)} %copy.15, s32[1024]{0:T(1024)S(1)} %pad_clamp_fusion), kind=kCustom, calls=%fused_computation | custom fusion | bytes 8390656 | tf_op jit(solution)/shard_map/jit(_take)/gather | solution.py:54
  248.1 0.0 copy-start.1
  248.1 7.7 %fusion.1 = f32[2048,512]{0,1:T(8,128)} fusion(f32[2048,512]{0,1:T(8,128)} %copy.14, f32[512,2048]{1,0:T(8,128)} %gather_fusion, bf16[2048,512]{0,1:T(8,128)(2,1)} %copy-done.2, pred[512]{0:T(512)(128)(4,1)S(1)} %get-tuple-element.8), kind=kLoop, calls=%fused_computation.3 | loop fusion | flops 5242880 | bytes 14680576 | tf_op jit(solution)/shard_map/add | solution.py:55
  255.8 5.3 %copy.19 = f32[2048,512]{1,0:T(8,128)} copy(f32[2048,512]{0,1:T(8,128)} %fusion.1) | data formatting | bytes 8388608
  261.1 0.0 copy-done.1
  (4 shorter events, 0.0 us)
Async XLA Ops:
  7.2 103.9 %copy-start = (bf16[512,2048]{1,0:T(8,128)(2,1)S(1)}, bf16[512,2048]{1,0:T(8,128)(2,1)}, u32[]{:S(2)}) copy-start(bf16[512,2048]{1,0:T(8,128)(2,1)} %param.13) | copy-start | bytes 6291460
  7.2 66.3 %reduce-scatter.2.cloned.1.call-start = ((), (), s32[]{:S(2)}) async-start(), calls=%async_computation.1 | async-start | bytes 5242880 | tf_op jit(solution)/shard_map/reduce_scatter | solution.py:16
  17.9 55.5 %copy-start.5 = (bf16[512,512]{1,0:T(8,128)(2,1)S(1)}, bf16[512,512]{1,0:T(8,128)(2,1)}, u32[]{:S(2)}) copy-start(bf16[512,512]{1,0:T(8,128)(2,1)} %param.11) | copy-start | bytes 1572868
  17.9 93.1 %all-gather.3.cloned.1.call-start = ((), (), s32[]{:S(2)}) async-start(), calls=%async_computation.2 | async-start | bytes 2621440 | tf_op jit(solution)/shard_map/all_gather | solution.py:26
  75.7 74.3 %all-gather.5.cloned.1.call-start = ((), (), s32[]{:S(2)}) async-start(), calls=%async_computation.3 | async-start | bytes 2621440 | tf_op jit(solution)/shard_map/all_gather | solution.py:33
  114.8 116.0 %all-reduce.2.cloned.1.call-start = ((), (), s32[]{:S(2)}) async-start(), calls=%async_computation.4 | async-start | bytes 4194304 | tf_op jit(solution)/shard_map/psum | solution.py:50
  118.9 5.6 %copy-start.3 = (bf16[2048,512]{1,0:T(8,128)(2,1)S(1)}, bf16[2048,512]{1,0:T(8,128)(2,1)}, u32[]{:S(2)}) copy-start(bf16[2048,512]{1,0:T(8,128)(2,1)} %param.10) | copy-start | bytes 6291460
  126.8 34.5 %copy-start.6 = (s32[512,1]{0,1:T(1,128)S(1)}, s32[512,1]{0,1:T(1,128)}, u32[]{:S(2)}) copy-start(s32[512,1]{0,1:T(1,128)} %param.15) | copy-start | bytes 6148
  126.8 34.5 %copy-start.7 = (f32[512]{0:T(512)S(1)}, f32[512]{0:T(512)}, u32[]{:S(2)}) copy-start(f32[512]{0:T(512)} %param.14) | copy-start | bytes 6148
  161.3 22.6 %copy-start.2 = (bf16[2048,512]{0,1:T(8,128)(2,1)}, bf16[2048,512]{0,1:T(8,128)(2,1)S(1)}, u32[]{:S(2)}) copy-start(bf16[2048,512]{0,1:T(8,128)(2,1)S(1)} %fusion.5) | copy-start | bytes 6291460
  162.7 20.2 %copy-start.4 = (bf16[512,512]{0,1:T(8,128)(2,1)S(1)}, bf16[512,512]{0,1:T(8,128)(2,1)}, u32[]{:S(2)}) copy-start(bf16[512,512]{0,1:T(8,128)(2,1)} %fusion.6) | copy-start | bytes 1572868
  248.1 13.0 %copy-start.1 = (bf16[512,2048]{1,0:T(8,128)(2,1)S(1)}, bf16[512,2048]{1,0:T(8,128)(2,1)}, u32[]{:S(2)}) copy-start(bf16[512,2048]{1,0:T(8,128)(2,1)} %param.13) | copy-start | bytes 6291460
Sparse Core Ops, SparseCore 0:
  18.1 55.3 reduce-scatter.1
  75.9 35.1 all-gather.2
  114.9 35.0 all-gather.4
  165.7 65.0 all-reduce.1
where the time goes:
time: 268 us
  waiting for transfers between devices  158 us (59%)
  local copies, waits for them, and re-layouts  33.8 us (13%)
  matrix products  30.4 us (11%)
  blocking collectives  16.8 us (6%)
  other arithmetic  14.1 us (5%)
  between operations  13.8 us (5%)
    reduce_scatter x1, waiting for transfers between devices, on_device(): lax.psum_scatter(lax.dot_general(columns, order_qty, contract_first, pref...  55.5 us
    psum x1, waiting for transfers between devices, on_device(): lax.psum(totals.astype(jnp.bfloat16), 'scen').astype(jnp.float32)  44.3 us
    all_gather x1, waiting for transfers between devices, on_device(): lax.all_gather(right_side, 'dec', axis=0, tiled=True)  35.4 us
    all_gather x1, waiting for transfers between devices, on_device(): lax.all_gather(recourse, 'dec', axis=0, tiled=True)  23.1 us
    unnamed x22, local copies, waits for them, and re-layouts  20.7 us
    psum x1, blocking collectives, on_device(): lax.psum(masses.astype(jnp.bfloat16), 'scen').astype(jnp.float32)  16.8 us
    dot_general x1, matrix products, on_device(): jnp.dot(columns, lax.all_gather(recourse, 'dec', axis=0, tiled=True), pre...  11.3 us
    dot_general x1, matrix products, on_device(): lax.dot_general(columns, order_qty, contract_first, preferred_element_typ...  10.7 us
  transfers between devices with their start and end apart: 4, of which 4 were waited for; matrix products, arithmetic and copies ran while one was open for 6% of the time, Pallas kernels for 0%

commit v1 on v0

--- a/solution.py
+++ b/solution.py
@@ -6,6 +6,12 @@
 G = 512
 step_size = 0.5
 penalty = 2.0
+
+
+def gather_and_add(block, name):
+    parts = lax.all_gather(block, name, axis=0, tiled=False)
+    total = parts.sum(axis=0)
+    return total
 
 
 def on_device(
@@ -47,7 +53,7 @@
     totals = totals + jnp.dot(planned, weight_low, preferred_element_type=jnp.float32)
     masses = jnp.dot(probability, member, precision=lax.Precision.HIGHEST)
     totals, masses = (
-        lax.psum(totals.astype(jnp.bfloat16), "scen").astype(jnp.float32),
+        gather_and_add(totals.astype(jnp.bfloat16), "scen").astype(jnp.float32),
         lax.psum(masses.astype(jnp.bfloat16), "scen").astype(jnp.float32),
     )
     consensus = totals / masses[None, :]

time: 268 us -> 366 us (1.37)
  waiting for transfers between devices: 158 us -> 244 us
  other arithmetic: 14.1 us -> 23 us
    all_gather x0 -> x1, waiting for transfers between devices: none -> 130 us  [gather_and_add(): parts = lax.all_gather(block, name, axis=0, tiled=False)]
    psum x1 -> x0, waiting for transfers between devices: 44.3 us -> none  [on_device(): lax.psum(totals.astype(jnp.bfloat16), 'scen').astype(jnp.float32)]
    reduce_sum x0 -> x1, other arithmetic: none -> 10.5 us  [gather_and_add(): total = parts.sum(axis=0)]
    div x1 -> x0, local copies, waits for them, and re-layouts: 5.46 us -> none  [on_device(): consensus = totals / masses[None, :]]
    unnamed x22 -> x23, local copies, waits for them, and re-layouts: 20.7 us -> 26.1 us
  transfers between devices with their start and end apart: 4 -> 4, of which waited for: 4 -> 4; matrix products, arithmetic and copies ran while one was open for 6% -> 4% of each run, Pallas kernels for 0% -> 0%
where the time goes in v1:
time: 366 us; the launch traced here: 365 us
  waiting for transfers between devices  244 us (67%)
  local copies, waits for them, and re-layouts  36.6 us (10%)
  matrix products  30.4 us (8%)
  other arithmetic  23 us (6%)
  blocking collectives  17 us (5%)
  between operations  13.9 us (4%)
    all_gather x1, waiting for transfers between devices, gather_and_add(): parts = lax.all_gather(block, name, axis=0, tiled=False)  130 us
    reduce_scatter x1, waiting for transfers between devices, on_device(): lax.psum_scatter(lax.dot_general(columns, order_qty, contract_first, pref...  55.5 us
    all_gather x1, waiting for transfers between devices, on_device(): lax.all_gather(right_side, 'dec', axis=0, tiled=True)  35.4 us
    unnamed x23, local copies, waits for them, and re-layouts  26.1 us
    all_gather x1, waiting for transfers between devices, on_device(): lax.all_gather(recourse, 'dec', axis=0, tiled=True)  23.1 us
    psum x1, blocking collectives, on_device(): lax.psum(masses.astype(jnp.bfloat16), 'scen').astype(jnp.float32)  17 us
    dot_general x1, matrix products, on_device(): jnp.dot(columns, lax.all_gather(recourse, 'dec', axis=0, tiled=True), pre...  11.3 us
    dot_general x1, matrix products, on_device(): lax.dot_general(columns, order_qty, contract_first, preferred_element_typ...  10.7 us
  transfers between devices with their start and end apart: 4, of which 4 were waited for; matrix products, arithmetic and copies ran while one was open for 4% of the time, Pallas kernels for 0%

profile of v1, /device:TPU:0, one launch (start us, length us, event | category | flops | bytes accessed | tf_op | source)
XLA Modules:
  0.0 365.4 jit_solution(17045630498027555449)
XLA Ops:
  7.2 0.0 copy-start
  7.2 0.0 reduce-scatter.2.cloned.1.call-start
  7.2 10.7 %fusion.20 = f32[2048,512]{1,0:T(8,128)} fusion(bf16[2048,2048]{1,0:T(8,128)(2,1)} %param.12, bf16[2048,512]{1,0:T(8,128)(2,1)} %param.8), kind=kOutput, calls=%fused_computation.32 | convolution fusion | flops 4294967296 | bytes 14680064 | tf_op jit(solution)/shard_map/dot_general | solution.py:23
  17.9 0.0 copy-start.5
  17.9 0.0 reduce-scatter.2.cloned.1.call-update
  17.9 0.0 all-gather.5.cloned.1.call-start
  18.0 55.5 %reduce-scatter.2.cloned.1.call-done = f32[512,512]{1,0:T(8,128)} async-done(((f32[2048,512]{1,0:T(8,128)}), f32[512,512]{1,0:T(8,128)}) %reduce-scatter.2.cloned.1.call-update) | async-done | bytes 1048592 | tf_op jit(solution)/shard_map/reduce_scatter | solution.py:22
  73.4 0.0 copy-done.5
  73.4 2.2 subtract_convert_fusion
  75.6 0.0 all-gather.5.cloned.1.call-update
  75.7 0.0 all-gather.7.cloned.1.call-start
  75.7 35.4 %all-gather.5.cloned.1.call-done = bf16[2048,512]{1,0:T(8,128)(2,1)} async-done(((bf16[512,512]{1,0:T(8,128)(2,1)}), bf16[2048,512]{1,0:T(8,128)(2,1)}) %all-gather.5.cloned.1.call-update) | async-done | bytes 2097168 | tf_op jit(solution)/shard_map/all_gather | solution.py:32
  111.1 0.0 copy-done
  111.1 3.7 %fusion.6 = bf16[512,512]{0,1:T(8,128)(2,1)} fusion(bf16[2048,512]{1,0:T(8,128)(2,1)} %all-gather.5.cloned.1.call-done, bf16[512,2048]{1,0:T(8,128)(2,1)S(1)} %copy-done), kind=kOutput, calls=%fused_computation.14 | convolution fusion | flops 1074003968 | bytes 4718592 | tf_op jit(solution)/shard_map/dot_general | solution.py:30
  114.7 0.0 all-gather.7.cloned.1.call-update
  114.8 0.2 all-gather.9.cloned.1.call-start
  115.0 3.9 %copy.20 = bf16[2048,512]{0,1:T(8,128)(2,1)} copy(bf16[2048,512]{1,0:T(8,128)(2,1)} %param.8) | data formatting | bytes 4194304 | tf_op args[0]
  118.9 0.0 copy-start.3
  118.9 5.6 %copy.22 = f32[2048,512]{0,1:T(8,128)} copy(f32[2048,512]{1,0:T(8,128)} %param.9) | data formatting | bytes 8388608 | tf_op args[1]
  124.5 0.0 copy-done.3
  124.5 2.4 copy.21
  126.8 0.0 copy-start.6
  126.8 0.0 copy-start.7
  126.9 23.1 %all-gather.7.cloned.1.call-done = bf16[2048,512]{0,1:T(8,128)(2,1)} async-done(((bf16[512,512]{0,1:T(8,128)(2,1)}), bf16[2048,512]{0,1:T(8,128)(2,1)}) %all-gather.7.cloned.1.call-update) | async-done | bytes 2097168 | tf_op jit(solution)/shard_map/all_gather | solution.py:39
  150.0 11.3 %fusion.5 = bf16[2048,512]{0,1:T(8,128)(2,1)S(1)} fusion(f32[2048,512]{0,1:T(8,128)} %copy.22, bf16[2048,512]{0,1:T(8,128)(2,1)} %copy.21, bf16[2048,512]{0,1:T(8,128)(2,1)} %copy.20, bf16[2048,512]{0,1:T(8,128)(2,1)} %all-gather.7.cloned.1.call-done, bf16[2048,2048]{1,0:T(8,128)(2,1)} %param.12), kind=kOutput, calls=%fused_computation.8 | convolution fusion | flops 4303355904 | bytes 20971520 | tf_op jit(solution)/shard_map/dot_general | solution.py:37
  161.3 0.0 copy-start.2
  161.3 0.0 copy-done.6
  161.3 0.0 copy-done.7
  161.3 1.4 fusion.9
  162.7 0.0 copy-start.4
  162.7 2.8 add_convert_fusion
  165.5 0.0 all-gather.9.cloned.1.call-update
  165.6 0.5 fusion.8
  166.1 17.0 %psum.7 = bf16[512]{0:T(512)(128)(2,1)S(1)} all-reduce(bf16[512]{0:T(512)(128)(2,1)S(1)} %convert_element_type.60), channel_id=1, replica_groups=mesh['scen'=8,'dec'=4] {'scen'}, use_global_device_ids=true, to_apply=%region_2.0 | all-reduce | flops 512 | bytes 2048 | tf_op jit(solution)/shard_map/psum | solution.py:57
  183.1 0.0 copy-done.4
  183.1 1.0 copy.26
  184.1 0.0 copy-done.2
  184.1 2.5 copy.25
  186.6 130.3 %all-gather.9.cloned.1.call-done = bf16[16384,512]{1,0:T(8,128)(2,1)} async-done(((bf16[2048,512]{1,0:T(8,128)(2,1)}), bf16[16384,512]{1,0:T(8,128)(2,1)}) %all-gather.9.cloned.1.call-update) | async-done | bytes 16777232 | tf_op jit(solution)/shard_map/all_gather | solution.py:12
  316.8 10.5 %reduce_sum.12 = bf16[2048,512]{1,0:T(8,128)(2,1)} reduce(bf16[8,2048,512]{2,1,0:T(8,128)(2,1)} %bitcast.32, bf16[]{:T(256)} %constant.20.clone.1), dimensions={0}, to_apply=%region_1.0 | reduce | flops 7340032 | bytes 18874370 | tf_op jit(solution)/shard_map/reduce_sum | solution.py:13
  327.4 2.9 copy.23
  330.3 2.5 convert_divide_fusion
  332.8 5.3 %copy.27 = f32[2048,512]{1,0:T(8,128)} copy(f32[2048,512]{0,1:T(8,128)} %convert_divide_fusion) | data formatting | bytes 8388608
  338.2 7.6 %gather_fusion = f32[512,2048]{1,0:T(8,128)} fusion(f32[2048,512]{0,1:T(8,128)} %convert_divide_fusion, s32[1024]{0:T(1024)S(1)} %pad_clamp_fusion), kind=kCustom, calls=%fused_computation | custom fusion | bytes 8390656 | tf_op jit(solution)/shard_map/jit(_take)/gather | solution.py:60
  345.8 0.0 copy-start.1
  345.8 7.7 %fusion.1 = f32[2048,512]{0,1:T(8,128)} fusion(f32[2048,512]{0,1:T(8,128)} %copy.22, f32[512,2048]{1,0:T(8,128)} %gather_fusion, bf16[2048,512]{0,1:T(8,128)(2,1)} %copy-done.2, pred[512]{0:T(512)(128)(4,1)S(1)} %get-tuple-element.12), kind=kLoop, calls=%fused_computation.3 | loop fusion | flops 5242880 | bytes 14680576 | tf_op jit(solution)/shard_map/add | solution.py:61
  353.5 5.3 %copy.28 = f32[2048,512]{1,0:T(8,128)} copy(f32[2048,512]{0,1:T(8,128)} %fusion.1) | data formatting | bytes 8388608
  358.8 0.0 copy-done.1
  (4 shorter events, 0.0 us)
Async XLA Ops:
  7.2 103.9 %copy-start = (bf16[512,2048]{1,0:T(8,128)(2,1)S(1)}, bf16[512,2048]{1,0:T(8,128)(2,1)}, u32[]{:S(2)}) copy-start(bf16[512,2048]{1,0:T(8,128)(2,1)} %param.13) | copy-start | bytes 6291460
  7.2 66.3 %reduce-scatter.2.cloned.1.call-start = ((), (), s32[]{:S(2)}) async-start(), calls=%async_computation.1 | async-start | bytes 5242880 | tf_op jit(solution)/shard_map/reduce_scatter | solution.py:22
  17.9 55.5 %copy-start.5 = (bf16[512,512]{1,0:T(8,128)(2,1)S(1)}, bf16[512,512]{1,0:T(8,128)(2,1)}, u32[]{:S(2)}) copy-start(bf16[512,512]{1,0:T(8,128)(2,1)} %param.11) | copy-start | bytes 1572868
  17.9 93.1 %all-gather.5.cloned.1.call-start = ((), (), s32[]{:S(2)}) async-start(), calls=%async_computation.2 | async-start | bytes 2621440 | tf_op jit(solution)/shard_map/all_gather | solution.py:32
  75.7 74.3 %all-gather.7.cloned.1.call-start = ((), (), s32[]{:S(2)}) async-start(), calls=%async_computation.3 | async-start | bytes 2621440 | tf_op jit(solution)/shard_map/all_gather | solution.py:39
  114.8 202.1 %all-gather.9.cloned.1.call-start = ((), (), s32[]{:S(2)}) async-start(), calls=%async_computation.4 | async-start | bytes 18874368 | tf_op jit(solution)/shard_map/all_gather | solution.py:12
  118.9 5.6 %copy-start.3 = (bf16[2048,512]{1,0:T(8,128)(2,1)S(1)}, bf16[2048,512]{1,0:T(8,128)(2,1)}, u32[]{:S(2)}) copy-start(bf16[2048,512]{1,0:T(8,128)(2,1)} %param.10) | copy-start | bytes 6291460
  126.8 34.5 %copy-start.6 = (s32[512,1]{0,1:T(1,128)S(1)}, s32[512,1]{0,1:T(1,128)}, u32[]{:S(2)}) copy-start(s32[512,1]{0,1:T(1,128)} %param.15) | copy-start | bytes 6148
  126.8 34.5 %copy-start.7 = (f32[512]{0:T(512)S(1)}, f32[512]{0:T(512)}, u32[]{:S(2)}) copy-start(f32[512]{0:T(512)} %param.14) | copy-start | bytes 6148
  161.3 22.8 %copy-start.2 = (bf16[2048,512]{0,1:T(8,128)(2,1)}, bf16[2048,512]{0,1:T(8,128)(2,1)S(1)}, u32[]{:S(2)}) copy-start(bf16[2048,512]{0,1:T(8,128)(2,1)S(1)} %fusion.5) | copy-start | bytes 6291460
  162.7 20.3 %copy-start.4 = (bf16[512,512]{0,1:T(8,128)(2,1)S(1)}, bf16[512,512]{0,1:T(8,128)(2,1)}, u32[]{:S(2)}) copy-start(bf16[512,512]{0,1:T(8,128)(2,1)} %fusion.6) | copy-start | bytes 1572868
  345.8 13.0 %copy-start.1 = (bf16[512,2048]{1,0:T(8,128)(2,1)S(1)}, bf16[512,2048]{1,0:T(8,128)(2,1)}, u32[]{:S(2)}) copy-start(bf16[512,2048]{1,0:T(8,128)(2,1)} %param.13) | copy-start | bytes 6291460
Sparse Core Ops, SparseCore 0:
  18.1 55.3 reduce-scatter.1
  75.9 35.1 all-gather.4
  114.9 35.0 all-gather.6
  165.7 151.1 all-gather.8
